TPU v7x, 256 devices: a whole 4x4x8 slice. The times are simulated.
256 devices in a mesh: clients: 32 (over z_hi, y, core), fsdp: 8 (over x, z_lo).
Axes of the slice: x: 4, y: 4, z: 8 (z_hi: 4, z_lo: 2; z = z_hi * 2 + z_lo), core: 2. Of those that a mesh axis runs over, the one named last changes fastest.
Arguments:
- token_ids: int32 [32, 5120], P('clients', 'fsdp'), may hold values from 0 to 16383
- target: bfloat16 [32, 5120, 768], P('clients', 'fsdp'), may hold values from -6 to 6
- embedding: bfloat16 [16384, 768], P(None, 'fsdp'), may hold values from -6 to 6
- norm_gain: float32 [768], replicated, may hold values from 0.1 to 1.9
- global_model: float32 [3, 768, 1024], P(None, 'fsdp', 'clients'), may hold values from -0.21875 to 0.21875
- global_control: float32 [3, 768, 1024], P(None, 'fsdp', 'clients'), may hold values from -140 to 140
- client_control: float32 [32, 3, 768, 1024], P('clients', None, 'fsdp'), may hold values from -150 to 150
- local_steps: int32 [32], replicated, may hold values from 1 to 2
- client_weight: int32 [32], replicated, may hold values from 1 to 4
Outputs:
- server_step: float32 [3, 768, 1024], P(None, 'fsdp', 'clients')
- server_control: float32 [3, 768, 1024], P(None, 'fsdp', 'clients')
- client_update: float32 [32, 3, 768, 1024], P('clients', None, 'fsdp')
All inputs are finite; a program needn't handle non-finite values.
Results may differ from a plain program's by a relative error of at most 0.025.
Values may be sent and summed in bfloat16 or wider, within the bound.
No kernel may reach another device: no remote copies, remote signals or barrier semaphores. Data moves between devices by JAX's collectives and lax.ppermute only.
A program may use at most 64 MiB of HBM per device.

v0:
```python
import math
import jax
import jax.numpy as jnp
from jax import lax
from jax.sharding import PartitionSpec as P

LOCAL = 2
learning_rate = 0.005
norm_eps = 1e-06


def copy_for_each(x, axis):
    size = lax.axis_size(axis)
    return lax.all_to_all(jnp.broadcast_to(x[None], (size, *x.shape)), axis, 0, 0, tiled=True)


def joined_along(pieces, dim):
    dims = list(pieces.shape[1:])
    dims[dim] *= pieces.shape[0]
    return jnp.moveaxis(pieces, 0, dim).reshape(dims)


def gathered_copies(x, axis, dim):
    pieces = copy_for_each(x, axis)
    return joined_along(pieces, dim)


def gather_turned(arrays, axis, dims):
    turned = [jnp.moveaxis(a, dim, 0) for a, dim in zip(arrays, dims)]
    widths = [t[0].size for t in turned]
    both = jnp.concatenate([t.reshape(-1, w) for t, w in zip(turned, widths)], axis=1)
    filled = lax.all_gather(both, axis, axis=0, tiled=True)
    pieces = jnp.split(filled, [sum(widths[:k]) for k in range(1, len(widths))], axis=1)
    return tuple(
        (
            jnp.moveaxis(b.reshape(-1, *t.shape[1:]), 0, dim)
            for b, t, dim in zip(pieces, turned, dims)
        )
    )


def cut_along(x, dim, size):
    before, after = (x.shape[:dim], x.shape[dim + 1 :])
    return jnp.moveaxis(x.reshape(*before, size, -1, *after), dim, 0)


def summed_on_arrival(x, axis, dim):
    pieces = cut_along(x, dim, lax.axis_size(axis))
    arrived = lax.all_to_all(pieces, axis, split_axis=0, concat_axis=0, tiled=True)
    return arrived.astype(jnp.float32).sum(axis=0)


def in_one_piece(arrays, axis, dim, along):
    ends, at = ([], 0)
    for a in arrays[:-1]:
        at += a.shape[along]
        ends.append(at)
    both = jnp.concatenate(arrays, axis=along)
    return tuple(
        jnp.split(lax.psum_scatter(both, axis, scatter_dimension=dim, tiled=True), ends, axis=along)
    )


def gelu_pair(pre_act):
    return jax.vjp(lambda inputs: jax.nn.gelu(inputs, approximate=True), pre_act)


def contract_rows(left, right):
    return lax.dot_general(
        left, right, (((0,), (0,)), ((), ())), preferred_element_type=jnp.float32
    )


def body(
    token_ids,
    target,
    embedding,
    norm_gain,
    global_model,
    global_control,
    client_control,
    local_steps,
    client_weight,
):
    tok_rows = target.shape[1]
    group_rows = tok_rows * lax.axis_size("fsdp")
    loss_scale = 1.0 / math.sqrt(group_rows)
    all_ids = gathered_copies(token_ids, "fsdp", 1)
    emb_columns = jnp.take(embedding, all_ids[0], axis=0)
    embedded = lax.all_to_all(emb_columns, "fsdp", split_axis=0, concat_axis=1, tiled=True)
    widened = embedded.astype(jnp.float32)
    inv_norm = lax.rsqrt(jnp.mean(widened * widened, axis=1, keepdims=True) + norm_eps)
    normed = (widened * inv_norm * norm_gain).astype(jnp.bfloat16)
    target_rows = target[0].astype(jnp.float32)
    model_rows, control_rows = tuple(
        (
            part.astype(jnp.float32)
            for part in gather_turned(
                (global_model.astype(jnp.bfloat16), global_control.astype(jnp.bfloat16)),
                "clients",
                (2, 2),
            )
        )
    )
    client_index = lax.axis_index("clients")
    slots = jnp.arange(local_steps.shape[0])
    step_count = jnp.sum(jnp.where(slots == client_index, local_steps, 0))
    own_weight = jnp.sum(jnp.where(slots == client_index, client_weight, 0)).astype(jnp.float32)
    weight_total = jnp.sum(client_weight).astype(jnp.float32)
    correction = control_rows - client_control[0]
    pseudo = jnp.zeros(model_rows.shape, jnp.float32)
    for local_step in range(LOCAL):
        current = (model_rows - learning_rate * pseudo).astype(jnp.bfloat16)
        gathered = lax.all_gather(current, "fsdp", axis=1, tiled=True)
        gate_pre = jnp.dot(normed, gathered[0], preferred_element_type=jnp.float32)
        up_pre = jnp.dot(normed, gathered[1], preferred_element_type=jnp.float32)
        gate_act, gelu_back = gelu_pair(gate_pre)
        hidden = (gate_act * up_pre).astype(jnp.bfloat16)
        projected = lax.dot_general(
            hidden, gathered[2], (((1,), (1,)), ((), ())), preferred_element_type=jnp.float32
        )
        out_grad = ((widened + projected - target_rows) * loss_scale).astype(jnp.bfloat16)
        hidden_grad = jnp.dot(out_grad, gathered[2], preferred_element_type=jnp.float32)
        gate_grad = gelu_back(hidden_grad * up_pre)[0].astype(jnp.bfloat16)
        up_grad = (hidden_grad * gate_act).astype(jnp.bfloat16)
        grad_terms = jnp.stack(
            [
                contract_rows(normed, gate_grad),
                contract_rows(normed, up_grad),
                contract_rows(out_grad, hidden),
            ]
        )
        grads = summed_on_arrival(grad_terms.astype(jnp.bfloat16), "fsdp", 1)
        step_mask = (local_step < step_count).astype(jnp.float32)
        pseudo = pseudo + step_mask * (grads + correction)
    update = client_control[0] - control_rows + pseudo / step_count.astype(jnp.float32)
    step_sum, control_sum = tuple(
        (
            part.astype(jnp.float32)
            for part in in_one_piece(
                (
                    (own_weight * pseudo).astype(jnp.bfloat16),
                    (own_weight * update).astype(jnp.bfloat16),
                ),
                "clients",
                2,
                0,
            )
        )
    )
    return (step_sum / weight_total, control_sum / weight_total, update[None])


def solution(mesh):
    placed = (
        P("clients", "fsdp"),
        P("clients", "fsdp", None),
        P(None, "fsdp"),
        P(),
        P(None, "fsdp", "clients"),
        P(None, "fsdp", "clients"),
        P("clients", None, "fsdp", None),
        P(),
        P(),
    )
    return jax.shard_map(
        body,
        mesh=mesh,
        in_specs=placed,
        out_specs=(
            P(None, "fsdp", "clients"),
            P(None, "fsdp", "clients"),
            P("clients", None, "fsdp", None),
        ),
        check_vma=False,
    )
```

profile of v0, /device:TPU:4, one launch (start us, length us, event | category | flops | bytes accessed | tf_op | source)
XLA Modules:
  0.0 550.3 jit_solution(11312081025137654549)
XLA Ops:
  7.2 0.8 convert_bitcast_fusion.2
  8.1 0.8 convert_bitcast_fusion.1
  9.1 0.7 pad_maximum_fusion.1
  9.8 56.8 %all-gather.4.cloned.1.call-done = bf16[1024,576]{1,0:T(8,128)(2,1)} async-done(((bf16[32,576]{1,0:T(8,128)(2,1)}), bf16[1024,576]{1,0:T(8,128)(2,1)}) %all-gather.4.cloned.1.call-update) | async-done | bytes 1179664 | tf_op jit(solution)/shard_map/all_gather | solution.py:32
  66.7 3.0 fusion.63
  69.6 2.2 copy.80
  71.9 0.6 broadcast_in_dim.30
  72.5 4.8 all-to-all-start
  77.3 3.9 copy.66
  81.3 16.5 %gather_fusion = bf16[5120,96]{1,0:T(8,128)(2,1)S(1)} fusion(bf16[16384,96]{1,0:T(8,128)(2,1)} %copy.66, s32[5120]{0:T(1024)S(1)} %broadcast_clamp_fusion), kind=kCustom, calls=%fused_computation | custom fusion | bytes 1986560 | tf_op jit(solution)/shard_map/jit(_take)/gather | solution.py:89
  97.8 0.7 copy.67
  98.5 1.1 broadcast_select_fusion
  99.6 5.8 %all-to-all-start.1 = ((bf16[8,640,96]{1,2,0:T(8,128)(2,1)}), bf16[8,640,96]{1,2,0:T(8,128)(2,1)S(1)}, u32[]{:S(2)}, u32[]{:S(2)}) async-start(bf16[8,640,96]{1,2,0:T(8,128)(2,1)} %broadcast_select_fusion), calls=%async_computation.1 | async-start | bytes 1966080 | tf_op jit(solution)/shard_map/all_to_all | solution.py:90
  105.4 23.6 %all-to-all-done.1 = bf16[8,640,96]{1,2,0:T(8,128)(2,1)S(1)} async-done(((bf16[8,640,96]{1,2,0:T(8,128)(2,1)}), bf16[8,640,96]{1,2,0:T(8,128)(2,1)S(1)}, u32[]{:S(2)}, u32[]{:S(2)}) %all-to-all-start.1) | async-done | bytes 983072 | tf_op jit(solution)/shard_map/all_to_all | solution.py:90
  129.2 1.8 copy.71
  131.8 50.4 %all-gather.6.cloned.1.call-done = bf16[3,768,1024]{2,1,0:T(8,128)(2,1)} async-done(((bf16[3,96,1024]{2,1,0:T(8,128)(2,1)}), bf16[3,768,1024]{2,1,0:T(8,128)(2,1)}) %all-gather.6.cloned.1.call-update) | async-done | bytes 4718608 | tf_op jit(solution)/shard_map/all_gather | solution.py:114
  182.2 2.8 fusion.21
  185.0 1.8 multiply_convert_fusion.3
  186.8 1.3 fusion.15
  188.1 1.4 convolution_convert_fusion.3
  189.5 1.2 fusion.26
  190.7 1.6 fusion.23
  192.3 2.7 fusion.22
  195.6 2.7 copy.72
  198.3 6.0 %all-to-all-start.2 = ((bf16[8,3,96,1024]{3,2,1,0:T(8,128)(2,1)}), bf16[8,3,96,1024]{3,2,1,0:T(8,128)(2,1)}, u32[]{:S(2)}, u32[]{:S(2)}) async-start(bf16[8,3,96,1024]{3,2,1,0:T(8,128)(2,1)} %copy.72), calls=%async_computation.2 | async-start | bytes 9437184 | tf_op jit(solution)/shard_map/all_to_all | solution.py:49
  204.4 0.6 fusion.40
  205.9 50.9 %all-to-all-done.2 = bf16[8,3,96,1024]{3,2,1,0:T(8,128)(2,1)} async-done(((bf16[8,3,96,1024]{3,2,1,0:T(8,128)(2,1)}), bf16[8,3,96,1024]{3,2,1,0:T(8,128)(2,1)}, u32[]{:S(2)}, u32[]{:S(2)}) %all-to-all-start.2) | async-done | bytes 4718624 | tf_op jit(solution)/shard_map/all_to_all | solution.py:49
  256.9 3.5 convert_reduce_fusion.1
  260.4 1.2 subtract_convert_fusion
  261.6 103.7 %all-gather.8.cloned.1.call-done = bf16[3,768,1024]{2,1,0:T(8,128)(2,1)} async-done(((bf16[3,96,1024]{2,1,0:T(8,128)(2,1)}), bf16[3,768,1024]{2,1,0:T(8,128)(2,1)}) %all-gather.8.cloned.1.call-update) | async-done | bytes 4718608 | tf_op jit(solution)/shard_map/all_gather | solution.py:114
  365.3 3.1 fusion.19
  368.7 1.8 multiply_convert_fusion.1
  370.5 1.3 fusion.17
  371.8 1.4 convolution_convert_fusion
  373.3 1.2 fusion.27
  374.5 1.5 fusion.25
  376.0 2.7 fusion.24
  379.3 2.7 copy.75
  382.1 6.0 %all-to-all-start.3 = ((bf16[8,3,96,1024]{3,2,1,0:T(8,128)(2,1)}), bf16[8,3,96,1024]{3,2,1,0:T(8,128)(2,1)}, u32[]{:S(2)}, u32[]{:S(2)}) async-start(bf16[8,3,96,1024]{3,2,1,0:T(8,128)(2,1)} %copy.75), calls=%async_computation.3 | async-start | bytes 9437184 | tf_op jit(solution)/shard_map/all_to_all | solution.py:49
  389.4 0.6 fusion.61
  390.6 49.9 %all-to-all-done.3 = bf16[8,3,96,1024]{3,2,1,0:T(8,128)(2,1)} async-done(((bf16[8,3,96,1024]{3,2,1,0:T(8,128)(2,1)}), bf16[8,3,96,1024]{3,2,1,0:T(8,128)(2,1)}, u32[]{:S(2)}, u32[]{:S(2)}) %all-to-all-start.3) | async-done | bytes 4718624 | tf_op jit(solution)/shard_map/all_to_all | solution.py:49
  440.6 3.5 convert_reduce_fusion
  444.1 1.6 multiply_convert_fusion.6
  445.8 2.8 copy.76
  449.2 92.3 %reduce-scatter.2.cloned.1.call-done = bf16[6,96,32]{1,0,2:T(8,128)(2,1)} async-done(((bf16[6,96,1024]{1,0,2:T(8,128)(2,1)}), bf16[6,96,32]{1,0,2:T(8,128)(2,1)}) %reduce-scatter.2.cloned.1.call-update) | async-done | bytes 36880 | tf_op jit(solution)/shard_map/reduce_scatter | solution.py:60
  541.5 0.9 convert_divide_fusion
  542.5 0.6 copy.78
  543.1 0.6 copy.77
  (63 shorter events, 3.3 us)
Async XLA Ops:
  7.2 59.5 %all-gather.4.cloned.1.call-start = ((), (), s32[]{:S(2)}) async-start(), calls=%async_computation.5 | async-start | bytes 1351680 | tf_op jit(solution)/shard_map/all_gather | solution.py:32
  9.1 62.8 %copy-start.11 = (s32[1,640]{1,0:T(1,128)S(1)}, s32[1,640]{1,0:T(1,128)}, u32[]{:S(2)}) copy-start(s32[1,640]{1,0:T(1,128)} %param.9) | copy-start | bytes 7684
  9.8 67.6 %copy-start.2 = (bf16[16384,96]{0,1:T(8,128)(2,1)S(1)}, bf16[16384,96]{0,1:T(8,128)(2,1)}, u32[]{:S(2)}) copy-start(bf16[16384,96]{0,1:T(8,128)(2,1)} %param.11) | copy-start | bytes 9437188
  9.8 172.4 %all-gather.6.cloned.1.call-start = ((), (), s32[]{:S(2)}) async-start(), calls=%async_computation.6 | async-start | bytes 5308416 | tf_op jit(solution)/shard_map/all_gather | solution.py:114
  72.5 8.8 %all-to-all-start = ((s32[8,1,640]{2,1,0:T(1,128)}), s32[8,1,640]{2,1,0:T(1,128)S(1)}, u32[]{:S(2)}, u32[]{:S(2)}) async-start(s32[8,1,640]{2,1,0:T(1,128)} %broadcast_in_dim.30), calls=%async_computation | async-start | bytes 40960 | tf_op jit(solution)/shard_map/all_to_all | solution.py:14
  97.8 7.5 %copy-start.10 = (f32[768]{0:T(1024)S(1)}, f32[768]{0:T(1024)}, u32[]{:S(2)}) copy-start(f32[768]{0:T(1024)} %param.12) | copy-start | bytes 9220
  99.6 29.5 %all-to-all-start.1 = ((bf16[8,640,96]{1,2,0:T(8,128)(2,1)}), bf16[8,640,96]{1,2,0:T(8,128)(2,1)S(1)}, u32[]{:S(2)}, u32[]{:S(2)}) async-start(bf16[8,640,96]{1,2,0:T(8,128)(2,1)} %broadcast_select_fusion), calls=%async_computation.1 | async-start | bytes 1966080 | tf_op jit(solution)/shard_map/all_to_all | solution.py:90
  131.5 60.8 %copy-start.6 = (bf16[640,768]{0,1:T(8,128)(2,1)}, bf16[640,768]{0,1:T(8,128)(2,1)S(1)}, u32[]{:S(2)}) copy-start(bf16[640,768]{0,1:T(8,128)(2,1)S(1)} %multiply_convert_fusion.5) | copy-start | bytes 2949124
  131.8 53.2 %copy-start.8 = (bf16[8,640,96]{1,2,0:T(8,128)(2,1)}, bf16[8,640,96]{1,2,0:T(8,128)(2,1)S(1)}, u32[]{:S(2)}) copy-start(bf16[8,640,96]{1,2,0:T(8,128)(2,1)S(1)} %multiply_convert_fusion.4) | copy-start | bytes 2949124
  182.2 2.8 copy-start.13
  185.0 1.8 copy-start.4
  185.0 1.8 copy-start.15
  198.3 6.0 %copy-start.17 = (s32[32]{0:T(128)S(1)}, s32[32]{0:T(128)}, u32[]{:S(2)}) copy-start(s32[32]{0:T(128)} %param.16) | copy-start | bytes 388
  198.3 7.3 %copy-start.3 = (bf16[1024,288]{1,0:T(8,128)(2,1)S(1)}, bf16[1024,288]{1,0:T(8,128)(2,1)}, u32[]{:S(2)}) copy-start(bf16[1024,288]{1,0:T(8,128)(2,1)} %get-tuple-element.26) | copy-start | bytes 1769476
  198.3 58.5 %all-to-all-start.2 = ((bf16[8,3,96,1024]{3,2,1,0:T(8,128)(2,1)}), bf16[8,3,96,1024]{3,2,1,0:T(8,128)(2,1)}, u32[]{:S(2)}, u32[]{:S(2)}) async-start(bf16[8,3,96,1024]{3,2,1,0:T(8,128)(2,1)} %copy.72), calls=%async_computation.2 | async-start | bytes 9437184 | tf_op jit(solution)/shard_map/all_to_all | solution.py:49
  204.3 160.9 %all-gather.8.cloned.1.call-start = ((), (), s32[]{:S(2)}) async-start(), calls=%async_computation.7 | async-start | bytes 5308416 | tf_op jit(solution)/shard_map/all_gather | solution.py:114
  205.9 54.4 %copy-start = (bf16[1024,288]{0,1:T(8,128)(2,1)S(1)}, bf16[1024,288]{0,1:T(8,128)(2,1)}, u32[]{:S(2)}) copy-start(bf16[1024,288]{0,1:T(8,128)(2,1)} %copy.80) | copy-start | bytes 1769476
  205.9 54.4 %copy-start.1 = (f32[1,3,96,1024]{3,2,1,0:T(8,128)S(1)}, f32[1,3,96,1024]{3,2,1,0:T(8,128)}, u32[]{:S(2)}) copy-start(f32[1,3,96,1024]{3,2,1,0:T(8,128)} %param.15) | copy-start | bytes 3538948
  365.3 3.1 copy-start.9
  365.3 3.4 copy-start.14
  368.7 1.8 copy-start.5
  368.7 1.8 copy-start.16
  373.3 1.2 copy-start.7
  382.1 7.3 %copy-start.12 = (s32[32]{0:T(128)S(1)}, s32[32]{0:T(128)}, u32[]{:S(2)}) copy-start(s32[32]{0:T(128)} %param.17) | copy-start | bytes 388
  382.1 58.5 %all-to-all-start.3 = ((bf16[8,3,96,1024]{3,2,1,0:T(8,128)(2,1)}), bf16[8,3,96,1024]{3,2,1,0:T(8,128)(2,1)}, u32[]{:S(2)}, u32[]{:S(2)}) async-start(bf16[8,3,96,1024]{3,2,1,0:T(8,128)(2,1)} %copy.75), calls=%async_computation.3 | async-start | bytes 9437184 | tf_op jit(solution)/shard_map/all_to_all | solution.py:49
  388.0 153.5 %reduce-scatter.2.cloned.1.call-start = ((), (), s32[]{:S(2)}) async-start(), calls=%async_computation.8 | async-start | bytes 2162688 | tf_op jit(solution)/shard_map/reduce_scatter | solution.py:60
Sparse Core Ops, SparseCore 0:
  11.1 55.5 all-gather.3
  72.0 110.1 all-gather.5
  261.7 103.5 all-gather.7
  448.7 92.7 reduce-scatter.1
where the time goes:
time: 551 us; the launch traced here: 550 us
  waiting for transfers between devices  428 us (78%)
  local copies, waits for them, and re-layouts  39.2 us (7%)
  matrix products  25.7 us (5%)
  starting transfers between devices  22.6 us (4%)
  other arithmetic  17.6 us (3%)
  between operations  17.4 us (3%)
    all_gather x2, waiting for transfers between devices, body(): gathered = lax.all_gather(current, 'fsdp', axis=1, tiled=True)  154 us
    all_to_all x2, waiting for transfers between devices, summed_on_arrival(): lax.all_to_all(pieces, axis, split_axis=0, concat_axis=0, tiled=True)  101 us
    reduce_scatter x1, waiting for transfers between devices, in_one_piece(): lax.psum_scatter(both, axis, scatter_dimension=dim, tiled=True)  92.3 us
    all_gather x1, waiting for transfers between devices, gather_turned(): filled = lax.all_gather(both, axis, axis=0, tiled=True)  56.8 us
    all_to_all x1, waiting for transfers between devices, body(): lax.all_to_all(emb_columns, 'fsdp', split_axis=0, concat_axis=1, tiled=True)  23.6 us
    gather x2, local copies, waits for them, and re-layouts, body(): emb_columns = jnp.take(embedding, all_ids[0], axis=0)  17.1 us
    all_to_all x2, starting transfers between devices, summed_on_arrival(): lax.all_to_all(pieces, axis, split_axis=0, concat_axis=0, tiled=True)  12 us
    dot_general x6, matrix products, contract_rows(): lax.dot_general(left, right, (((0,), (0,)), ((), ())), preferred_element_...  11.4 us
  transfers between devices with their start and end apart: 8, of which 7 were waited for; matrix products, arithmetic and copies ran while one was open for 5% of the time, Pallas kernels for 0%

commit v1 on v0

--- a/solution.py
+++ b/solution.py
@@ -87,7 +87,12 @@
     loss_scale = 1.0 / math.sqrt(group_rows)
     all_ids = gathered_copies(token_ids, "fsdp", 1)
     emb_columns = jnp.take(embedding, all_ids[0], axis=0)
-    embedded = lax.all_to_all(emb_columns, "fsdp", split_axis=0, concat_axis=1, tiled=True)
+    embedded = jnp.concatenate(
+        lax.all_to_all(
+            jnp.stack(jnp.split(emb_columns, lax.axis_size("fsdp"), axis=0)), "fsdp", 0, 0
+        ),
+        axis=1,
+    )
     widened = embedded.astype(jnp.float32)
     inv_norm = lax.rsqrt(jnp.mean(widened * widened, axis=1, keepdims=True) + norm_eps)
     normed = (widened * inv_norm * norm_gain).astype(jnp.bfloat16)

time: 551 us -> 551 us (level)
    gather x2 -> x1, local copies, waits for them, and re-layouts: 17.1 us -> 16.5 us  [body(): emb_columns = jnp.take(embedding, all_ids[0], axis=0)]
where the time goes in v1:
time: 551 us; the launch traced here: 550 us
  waiting for transfers between devices  425 us (77%)
  local copies, waits for them, and re-layouts  40.1 us (7%)
  matrix products  25.7 us (5%)
  starting transfers between devices  22.6 us (4%)
  other arithmetic  19.2 us (3%)
  between operations  17.4 us (3%)
    all_gather x2, waiting for transfers between devices, body(): gathered = lax.all_gather(current, 'fsdp', axis=1, tiled=True)  152 us
    all_to_all x2, waiting for transfers between devices, summed_on_arrival(): lax.all_to_all(pieces, axis, split_axis=0, concat_axis=0, tiled=True)  101 us
    reduce_scatter x1, waiting for transfers between devices, in_one_piece(): lax.psum_scatter(both, axis, scatter_dimension=dim, tiled=True)  92.3 us
    all_gather x1, waiting for transfers between devices, gather_turned(): filled = lax.all_gather(both, axis, axis=0, tiled=True)  56.8 us
    all_to_all x1, waiting for transfers between devices, body(): lax.all_to_all(jnp.stack(jnp.split(emb_columns, lax.axis_size('fsdp'), ax...  23.6 us
    gather x1, local copies, waits for them, and re-layouts, body(): emb_columns = jnp.take(embedding, all_ids[0], axis=0)  16.5 us
    all_to_all x2, starting transfers between devices, summed_on_arrival(): lax.all_to_all(pieces, axis, split_axis=0, concat_axis=0, tiled=True)  12 us
    dot_general x6, matrix products, contract_rows(): lax.dot_general(left, right, (((0,), (0,)), ((), ())), preferred_element_...  11.4 us
  transfers between devices with their start and end apart: 8, of which 7 were waited for; matrix products, arithmetic and copies ran while one was open for 5% of the time, Pallas kernels for 0%

profile of v1, /device:TPU:4, one launch (start us, length us, event | category | flops | bytes accessed | tf_op | source)
XLA Modules:
  0.0 550.3 jit_solution(8721858508441281512)
XLA Ops:
  7.2 0.8 convert_bitcast_fusion.2
  8.1 0.8 convert_bitcast_fusion.1
  9.1 0.7 pad_maximum_fusion.1
  9.8 56.8 %all-gather.4.cloned.1.call-done = bf16[1024,576]{1,0:T(8,128)(2,1)} async-done(((bf16[32,576]{1,0:T(8,128)(2,1)}), bf16[1024,576]{1,0:T(8,128)(2,1)}) %all-gather.4.cloned.1.call-update) | async-done | bytes 1179664 | tf_op jit(solution)/shard_map/all_gather | solution.py:32
  66.7 3.0 fusion.71
  69.6 2.2 copy.81
  71.9 0.6 broadcast_in_dim.30
  72.5 4.8 all-to-all-start
  77.3 3.9 copy.68
  81.3 16.5 %gather_fusion = bf16[5120,96]{1,0:T(8,128)(2,1)S(1)} fusion(bf16[16384,96]{1,0:T(8,128)(2,1)} %copy.68, s32[5120]{0:T(1024)S(1)} %broadcast_clamp_fusion), kind=kCustom, calls=%fused_computation | custom fusion | bytes 1986560 | tf_op jit(solution)/shard_map/jit(_take)/gather | solution.py:89
  97.8 2.7 broadcast_select_fusion
  100.7 1.4 copy.69
  102.1 5.8 %all-to-all-start.1 = ((bf16[8,640,96]{1,2,0:T(8,128)(2,1)}), bf16[8,640,96]{1,2,0:T(8,128)(2,1)S(1)}, u32[]{:S(2)}, u32[]{:S(2)}) async-start(bf16[8,640,96]{1,2,0:T(8,128)(2,1)} %copy.69), calls=%async_computation.1 | async-start | bytes 1966080 | tf_op jit(solution)/shard_map/all_to_all | solution.py:91
  107.9 23.6 %all-to-all-done.1 = bf16[8,640,96]{1,2,0:T(8,128)(2,1)S(1)} async-done(((bf16[8,640,96]{1,2,0:T(8,128)(2,1)}), bf16[8,640,96]{1,2,0:T(8,128)(2,1)S(1)}, u32[]{:S(2)}, u32[]{:S(2)}) %all-to-all-start.1) | async-done | bytes 983072 | tf_op jit(solution)/shard_map/all_to_all | solution.py:91
  131.7 1.8 copy.73
  134.4 47.8 %all-gather.6.cloned.1.call-done = bf16[3,768,1024]{2,1,0:T(8,128)(2,1)} async-done(((bf16[3,96,1024]{2,1,0:T(8,128)(2,1)}), bf16[3,768,1024]{2,1,0:T(8,128)(2,1)}) %all-gather.6.cloned.1.call-update) | async-done | bytes 4718608 | tf_op jit(solution)/shard_map/all_gather | solution.py:119
  182.2 2.8 fusion.21
  185.0 1.8 multiply_convert_fusion.3
  186.8 1.3 fusion.15
  188.1 1.4 convolution_convert_fusion.3
  189.5 1.2 fusion.26
  190.7 1.6 fusion.23
  192.3 2.7 fusion.22
  195.6 2.7 copy.74
  198.3 6.0 %all-to-all-start.2 = ((bf16[8,3,96,1024]{3,2,1,0:T(8,128)(2,1)}), bf16[8,3,96,1024]{3,2,1,0:T(8,128)(2,1)}, u32[]{:S(2)}, u32[]{:S(2)}) async-start(bf16[8,3,96,1024]{3,2,1,0:T(8,128)(2,1)} %copy.74), calls=%async_computation.2 | async-start | bytes 9437184 | tf_op jit(solution)/shard_map/all_to_all | solution.py:49
  204.4 0.6 fusion.48
  205.9 50.9 %all-to-all-done.2 = bf16[8,3,96,1024]{3,2,1,0:T(8,128)(2,1)} async-done(((bf16[8,3,96,1024]{3,2,1,0:T(8,128)(2,1)}), bf16[8,3,96,1024]{3,2,1,0:T(8,128)(2,1)}, u32[]{:S(2)}, u32[]{:S(2)}) %all-to-all-start.2) | async-done | bytes 4718624 | tf_op jit(solution)/shard_map/all_to_all | solution.py:49
  256.9 3.5 convert_reduce_fusion.1
  260.4 1.2 subtract_convert_fusion
  261.6 103.7 %all-gather.8.cloned.1.call-done = bf16[3,768,1024]{2,1,0:T(8,128)(2,1)} async-done(((bf16[3,96,1024]{2,1,0:T(8,128)(2,1)}), bf16[3,768,1024]{2,1,0:T(8,128)(2,1)}) %all-gather.8.cloned.1.call-update) | async-done | bytes 4718608 | tf_op jit(solution)/shard_map/all_gather | solution.py:119
  365.3 3.1 fusion.19
  368.7 1.8 multiply_convert_fusion.1
  370.5 1.3 fusion.17
  371.8 1.4 convolution_convert_fusion
  373.3 1.2 fusion.27
  374.5 1.5 fusion.25
  376.0 2.7 fusion.24
  379.3 2.7 copy.77
  382.1 6.0 %all-to-all-start.3 = ((bf16[8,3,96,1024]{3,2,1,0:T(8,128)(2,1)}), bf16[8,3,96,1024]{3,2,1,0:T(8,128)(2,1)}, u32[]{:S(2)}, u32[]{:S(2)}) async-start(bf16[8,3,96,1024]{3,2,1,0:T(8,128)(2,1)} %copy.77), calls=%async_computation.3 | async-start | bytes 9437184 | tf_op jit(solution)/shard_map/all_to_all | solution.py:49
  389.4 0.6 fusion.69
  390.6 49.9 %all-to-all-done.3 = bf16[8,3,96,1024]{3,2,1,0:T(8,128)(2,1)} async-done(((bf16[8,3,96,1024]{3,2,1,0:T(8,128)(2,1)}), bf16[8,3,96,1024]{3,2,1,0:T(8,128)(2,1)}, u32[]{:S(2)}, u32[]{:S(2)}) %all-to-all-start.3) | async-done | bytes 4718624 | tf_op jit(solution)/shard_map/all_to_all | solution.py:49
  440.6 3.5 convert_reduce_fusion
  444.1 1.6 multiply_convert_fusion.6
  445.8 2.8 copy.78
  449.2 92.3 %reduce-scatter.2.cloned.1.call-done = bf16[6,96,32]{1,0,2:T(8,128)(2,1)} async-done(((bf16[6,96,1024]{1,0,2:T(8,128)(2,1)}), bf16[6,96,32]{1,0,2:T(8,128)(2,1)}) %reduce-scatter.2.cloned.1.call-update) | async-done | bytes 36880 | tf_op jit(solution)/shard_map/reduce_scatter | solution.py:60
  541.5 0.9 convert_divide_fusion
  542.5 0.6 copy.80
  543.1 0.6 copy.79
  (71 shorter events, 3.5 us)
Async XLA Ops:
  7.2 59.5 %all-gather.4.cloned.1.call-start = ((), (), s32[]{:S(2)}) async-start(), calls=%async_computation.5 | async-start | bytes 1351680 | tf_op jit(solution)/shard_map/all_gather | solution.py:32
  9.1 62.8 %copy-start.11 = (s32[1,640]{1,0:T(1,128)S(1)}, s32[1,640]{1,0:T(1,128)}, u32[]{:S(2)}) copy-start(s32[1,640]{1,0:T(1,128)} %param.9) | copy-start | bytes 7684
  9.8 67.6 %copy-start.2 = (bf16[16384,96]{0,1:T(8,128)(2,1)S(1)}, bf16[16384,96]{0,1:T(8,128)(2,1)}, u32[]{:S(2)}) copy-start(bf16[16384,96]{0,1:T(8,128)(2,1)} %param.11) | copy-start | bytes 9437188
  9.8 172.4 %all-gather.6.cloned.1.call-start = ((), (), s32[]{:S(2)}) async-start(), calls=%async_computation.6 | async-start | bytes 5308416 | tf_op jit(solution)/shard_map/all_gather | solution.py:119
  72.5 8.8 %all-to-all-start = ((s32[8,1,640]{2,1,0:T(1,128)}), s32[8,1,640]{2,1,0:T(1,128)S(1)}, u32[]{:S(2)}, u32[]{:S(2)}) async-start(s32[8,1,640]{2,1,0:T(1,128)} %broadcast_in_dim.30), calls=%async_computation | async-start | bytes 40960 | tf_op jit(solution)/shard_map/all_to_all | solution.py:14
  100.6 7.2 %copy-start.10 = (f32[768]{0:T(1024)S(1)}, f32[768]{0:T(1024)}, u32[]{:S(2)}) copy-start(f32[768]{0:T(1024)} %param.12) | copy-start | bytes 9220
  102.1 29.5 %all-to-all-start.1 = ((bf16[8,640,96]{1,2,0:T(8,128)(2,1)}), bf16[8,640,96]{1,2,0:T(8,128)(2,1)S(1)}, u32[]{:S(2)}, u32[]{:S(2)}) async-start(bf16[8,640,96]{1,2,0:T(8,128)(2,1)} %copy.69), calls=%async_computation.1 | async-start | bytes 1966080 | tf_op jit(solution)/shard_map/all_to_all | solution.py:91
  134.1 58.2 %copy-start.6 = (bf16[640,768]{0,1:T(8,128)(2,1)}, bf16[640,768]{0,1:T(8,128)(2,1)S(1)}, u32[]{:S(2)}) copy-start(bf16[640,768]{0,1:T(8,128)(2,1)S(1)} %multiply_convert_fusion.5) | copy-start | bytes 2949124
  134.4 50.6 %copy-start.8 = (bf16[8,640,96]{1,2,0:T(8,128)(2,1)}, bf16[8,640,96]{1,2,0:T(8,128)(2,1)S(1)}, u32[]{:S(2)}) copy-start(bf16[8,640,96]{1,2,0:T(8,128)(2,1)S(1)} %multiply_convert_fusion.4) | copy-start | bytes 2949124
  182.2 2.8 copy-start.13
  185.0 1.8 copy-start.4
  185.0 1.8 copy-start.15
  198.3 6.0 %copy-start.17 = (s32[32]{0:T(128)S(1)}, s32[32]{0:T(128)}, u32[]{:S(2)}) copy-start(s32[32]{0:T(128)} %param.16) | copy-start | bytes 388
  198.3 7.3 %copy-start.3 = (bf16[1024,288]{1,0:T(8,128)(2,1)S(1)}, bf16[1024,288]{1,0:T(8,128)(2,1)}, u32[]{:S(2)}) copy-start(bf16[1024,288]{1,0:T(8,128)(2,1)} %get-tuple-element.26) | copy-start | bytes 1769476
  198.3 58.5 %all-to-all-start.2 = ((bf16[8,3,96,1024]{3,2,1,0:T(8,128)(2,1)}), bf16[8,3,96,1024]{3,2,1,0:T(8,128)(2,1)}, u32[]{:S(2)}, u32[]{:S(2)}) async-start(bf16[8,3,96,1024]{3,2,1,0:T(8,128)(2,1)} %copy.74), calls=%async_computation.2 | async-start | bytes 9437184 | tf_op jit(solution)/shard_map/all_to_all | solution.py:49
  204.3 160.9 %all-gather.8.cloned.1.call-start = ((), (), s32[]{:S(2)}) async-start(), calls=%async_computation.7 | async-start | bytes 5308416 | tf_op jit(solution)/shard_map/all_gather | solution.py:119
  205.9 54.4 %copy-start = (bf16[1024,288]{0,1:T(8,128)(2,1)S(1)}, bf16[1024,288]{0,1:T(8,128)(2,1)}, u32[]{:S(2)}) copy-start(bf16[1024,288]{0,1:T(8,128)(2,1)} %copy.81) | copy-start | bytes 1769476
  205.9 54.4 %copy-start.1 = (f32[1,3,96,1024]{3,2,1,0:T(8,128)S(1)}, f32[1,3,96,1024]{3,2,1,0:T(8,128)}, u32[]{:S(2)}) copy-start(f32[1,3,96,1024]{3,2,1,0:T(8,128)} %param.15) | copy-start | bytes 3538948
  365.3 3.1 copy-start.9
  365.3 3.4 copy-start.14
  368.7 1.8 copy-start.5
  368.7 1.8 copy-start.16
  373.3 1.2 copy-start.7
  382.1 7.3 %copy-start.12 = (s32[32]{0:T(128)S(1)}, s32[32]{0:T(128)}, u32[]{:S(2)}) copy-start(s32[32]{0:T(128)} %param.17) | copy-start | bytes 388
  382.1 58.5 %all-to-all-start.3 = ((bf16[8,3,96,1024]{3,2,1,0:T(8,128)(2,1)}), bf16[8,3,96,1024]{3,2,1,0:T(8,128)(2,1)}, u32[]{:S(2)}, u32[]{:S(2)}) async-start(bf16[8,3,96,1024]{3,2,1,0:T(8,128)(2,1)} %copy.77), calls=%async_computation.3 | async-start | bytes 9437184 | tf_op jit(solution)/shard_map/all_to_all | solution.py:49
  388.0 153.5 %reduce-scatter.2.cloned.1.call-start = ((), (), s32[]{:S(2)}) async-start(), calls=%async_computation.8 | async-start | bytes 2162688 | tf_op jit(solution)/shard_map/reduce_scatter | solution.py:60
Sparse Core Ops, SparseCore 0:
  11.1 55.5 all-gather.3
  72.0 110.1 all-gather.5
  261.7 103.5 all-gather.7
  448.7 92.7 reduce-scatter.1
